TPU v7x, 128 devices: a whole 4x4x4 slice. The times are simulated.
128 devices in a mesh: dp: 16 (over z, x), tm: 8 (over y, core).
Axes of the slice: x: 4, y: 4, z: 4, core: 2. Of those that a mesh axis runs over, the one named last changes fastest.
Arguments:
- frames: bfloat16 [16, 6144, 1024], P('dp', 'tm'), may hold values from -18 to 18
- lengths: int32 [16], P('dp'), may hold values from 1 to 6144, 58982 in all
- w_in: bfloat16 [1024, 2048], replicated, may hold values from -4 to 4
- w_dw: float32 [31, 1024], replicated, may hold values from -1 to 1
- bn_gain: float32 [1024], replicated, may hold values from 0.25 to 1.75
- bn_bias: float32 [1024], replicated, may hold values from -1 to 1
- w_out: bfloat16 [1024, 1024], replicated, may hold values from -0.1875 to 0.1875
- cotangent: bfloat16 [16, 6144, 1024], P('dp', 'tm'), may hold values from -6 to 6
Outputs:
- output: bfloat16 [16, 6144, 1024], P('dp', 'tm')
- grad_frames: bfloat16 [16, 6144, 1024], P('dp', 'tm')
- grad_w_in: float32 [1024, 2048], P(('dp', 'tm'))
- grad_w_out: float32 [1024, 1024], P(('dp', 'tm'))
- grad_kernel: float32 [31, 1024], replicated
- grad_gain: float32 [1024], replicated
- grad_bias: float32 [1024], replicated
Inputs may be any that keep to these rules, and one draw needn't show every extreme that they name: Frame slots at or after a recording's length are padding; the lengths sum to 58982 and the longest is exactly 6144.
All inputs are finite; a program needn't handle non-finite values. No bound on the sum of `lengths` on one device may be relied on, other than what follows from the above.
Results may differ from a plain program's by a relative error of at most 0.015.
Values may be sent and summed in bfloat16 or wider, within the bound.
A program may use at most 128 MiB of HBM per device.

v0:
```python
import math
import jax
import jax.numpy as jnp
from jax import lax
from jax.sharding import PartitionSpec as P


def padded_2(cells, sides, width):
    for axis, dim in sides:
        count = lax.axis_size(axis)
        ends = count - 1
        head = lax.slice_in_dim(cells, 0, width, axis=dim)
        tail = lax.slice_in_dim(cells, cells.shape[dim] - width, cells.shape[dim], axis=dim)
        cells = jnp.concatenate(
            [
                lax.ppermute(tail, axis, [(i, (i + 1) % count) for i in range(ends)]),
                cells,
                lax.ppermute(head, axis, [((i + 1) % count, i) for i in range(ends)]),
            ],
            axis=dim,
        )
    return cells


def taps_forward(padded, kernel, frame_count):
    summed = jnp.zeros((frame_count, padded.shape[1]), jnp.float32)
    for tap_index in range(kernel.shape[0]):
        summed = summed + kernel[tap_index] * padded[tap_index : tap_index + frame_count].astype(
            jnp.float32
        )
    return summed


def taps_backward(padded_grad, kernel, frame_count):
    reach_both = kernel.shape[0] - 1
    summed = jnp.zeros((frame_count, padded_grad.shape[1]), jnp.float32)
    for tap_index in range(kernel.shape[0]):
        begin = reach_both - tap_index
        summed = summed + kernel[tap_index] * padded_grad[begin : begin + frame_count].astype(
            jnp.float32
        )
    return summed


def taps_kernel(padded_glu, dconv_rows, kernel_taps, frame_count):
    grad_rows = dconv_rows.astype(jnp.float32)
    tap_rows = []
    for tap_index in range(kernel_taps):
        tap_rows.append(
            jnp.sum(
                padded_glu[tap_index : tap_index + frame_count].astype(jnp.float32) * grad_rows,
                axis=0,
            )
        )
    return jnp.stack(tap_rows)


def row_product(left_rows, right_mat, contract):
    dim_spec = (((1,), (contract,)), ((), ()))
    return lax.dot_general(left_rows, right_mat, dim_spec, preferred_element_type=jnp.float32)


def local(frames, lengths, w_in, w_dw, bn_gain, bn_bias, w_out, cotangent):
    frame_rows = frames.shape[1]
    channels = frames.shape[2]
    kernel_taps = w_dw.shape[0]
    reach = (kernel_taps - 1) // 2
    feats = frames[0]
    cot_rows = cotangent[0]
    tm_count = lax.axis_size("tm")
    device_count = lax.axis_size("dp") * tm_count
    offset = lax.axis_index("tm") * frame_rows
    limit = lengths[0]
    positions = offset + jnp.arange(frame_rows, dtype=jnp.int32)
    live_rows = (positions < limit).astype(jnp.float32)[:, None]
    contract_frames = (((0,), (0,)), ((), ()))
    pre_act = row_product(feats, w_in, 0)
    linear_half = pre_act[:, :channels]
    gate_sig = jax.nn.sigmoid(pre_act[:, channels:])
    glu_out = (linear_half * gate_sig * live_rows).astype(jnp.bfloat16)
    dswish = row_product(cot_rows, w_out, 1)
    padded = padded_2(glu_out, (("tm", 0),), reach)
    conv_out = taps_forward(padded, w_dw, frame_rows)
    local_sum = jnp.sum(conv_out * live_rows, axis=0)
    local_sq = jnp.sum(conv_out * conv_out * live_rows, axis=0)
    local_count = jnp.sum(live_rows)
    sums, squares, count = lax.psum((local_sum, local_sq, local_count), ("dp", "tm"))
    mean_vec = sums / count
    variance = squares / count - mean_vec * mean_vec
    inv_std = lax.rsqrt(variance + 1e-05)
    normed = (conv_out - mean_vec) * inv_std
    shifted = bn_gain * normed + bn_bias
    act_sig = jax.nn.sigmoid(shifted)
    swished = (shifted * act_sig * live_rows).astype(jnp.bfloat16)
    dshift = live_rows * dswish * act_sig * (1.0 + shifted * (1.0 - act_sig))
    sum_gain, sum_bias = lax.psum(
        (jnp.sum(dshift * normed, axis=0), jnp.sum(dshift, axis=0)), ("dp", "tm")
    )
    dconv = (
        live_rows * bn_gain * inv_std * (dshift - sum_bias / count - normed * sum_gain / count)
    ).astype(jnp.bfloat16)
    padded_grad = padded_2(dconv, (("tm", 0),), reach)
    dglu = live_rows * taps_backward(padded_grad, w_dw, frame_rows)
    kernel_sum = lax.psum(taps_kernel(padded, dconv, kernel_taps, frame_rows), ("dp", "tm"))
    out_rows = row_product(swished, w_out, 0).astype(jnp.bfloat16)
    dpre = jnp.concatenate(
        [dglu * gate_sig, dglu * linear_half * gate_sig * (1.0 - gate_sig)], axis=1
    ).astype(jnp.bfloat16)
    grad_rows = row_product(dpre, w_in, 1).astype(jnp.bfloat16)
    term_in = lax.dot_general(feats, dpre, contract_frames, preferred_element_type=jnp.float32)
    term_out = lax.dot_general(
        swished, cot_rows, contract_frames, preferred_element_type=jnp.float32
    )
    weight_term = jnp.concatenate([term_in, term_out], axis=1)
    weight_sum = lax.psum_scatter(weight_term, ("dp", "tm"), scatter_dimension=0, tiled=True)
    scale = 1.0 / math.sqrt(device_count * frame_rows)
    grad_w_in = weight_sum[:, : 2 * channels] * scale
    grad_w_out = weight_sum[:, 2 * channels :] * scale
    return (
        out_rows[None],
        grad_rows[None],
        grad_w_in,
        grad_w_out,
        kernel_sum * scale,
        sum_gain * scale,
        sum_bias * scale,
    )


def solution(mesh):
    placed = (P("dp", "tm", None), P("dp"), P(), P(), P(), P(), P(), P("dp", "tm", None))
    return jax.shard_map(
        local,
        mesh=mesh,
        in_specs=placed,
        out_specs=(
            P("dp", "tm", None),
            P("dp", "tm", None),
            P(("dp", "tm"), None),
            P(("dp", "tm"), None),
            P(),
            P(),
            P(),
        ),
        check_vma=False,
    )
```

profile of v0, /device:TPU:0, one launch (start us, length us, event | category | flops | bytes accessed | tf_op | source)
XLA Modules:
  0.0 603.7 jit_solution(6638876811179374699)
XLA Ops:
  8.0 5.7 fusion.143
  19.8 3.0 collective-permute-done.1
  22.8 24.4 %multiply_reduce_fusion.2 = (f32[1024]{0:T(1024)S(1)}, f32[1024]{0:T(1024)S(1)}, f32[768,1024]{1,0:T(8,128)}) fusion(f32[768]{0:T(1024)S(1)} %fusion.147, bf16[15,1024]{1,0:T(8,128)(2,1)S(1)} %collective-permute-done.1, bf16[768,1024]{1,0:T(8,128)(2,1)S(1)} %multiply_convert_fusion.4, f32[1024]{0:T(1024)S(1)} %bitcast.146, f32[1024]{0:T(1024)S(1)} %bitcast.148, ...), kind=kLoop, calls=%fused_computation.213 | loop fusion | flops 147060736 | bytes 4918272 | tf_op jit(solution)/shard_map/reduce_sum | solution.py:84
  47.2 69.6 %all-reduce.1 = (f32[1024]{0:T(1024)S(1)}, f32[]{:T(128)}, f32[1024]{0:T(1024)S(1)}) all-reduce(f32[1024]{0:T(1024)S(1)} %get-tuple-element.52, f32[]{:T(128)} %fusion.148, f32[1024]{0:T(1024)S(1)} %get-tuple-element.51), channel_id=1, replica_groups=mesh['dp'=16,'tm'=8] {'dp','tm'}, use_global_device_ids=true, to_apply=%region_5.0 | all-reduce | flops 2049 | bytes 16392 | tf_op jit(solution)/shard_map/psum | solution.py:87
  117.6 6.4 %fusion.151 = (f32[1024]{0:T(1024)S(1)}, f32[1024]{0:T(1024)S(1)}, f32[768,1024]{1,0:T(8,128)}) fusion(f32[1024]{0:T(1024)S(1)} %get-tuple-element.106, f32[768,1024]{1,0:T(8,128)} %get-tuple-element.67, f32[1024]{0:T(1024)S(1)} %get-tuple-element.105, f32[1024]{0:T(1024)S(1)} %copy-done.16, f32[1024]{0:T(1024)S(1)} %copy-done.12, ...), kind=kOutput, calls=%fused_computation.316 | convolution fusion | flops 1623193600 | bytes 9989120 | tf_op jit(solution)/shard_map/dot_general | solution.py:60
  124.0 63.8 %all-reduce = (f32[1024]{0:T(1024)S(1)}, f32[1024]{0:T(1024)S(1)}) all-reduce(f32[1024]{0:T(1024)S(1)} %get-tuple-element.58, f32[1024]{0:T(1024)S(1)} %get-tuple-element.57), channel_id=1, replica_groups=mesh['dp'=16,'tm'=8] {'dp','tm'}, use_global_device_ids=true, to_apply=%region_9.0 | all-reduce | flops 2048 | bytes 16384 | tf_op jit(solution)/shard_map/psum | solution.py:96
  189.0 15.0 %fusion.75 = (f32[1024]{0:T(1024)S(1)}, f32[1024]{0:T(1024)S(1)}, f32[1024]{0:T(1024)S(1)}, f32[1024]{0:T(1024)S(1)}, f32[1024]{0:T(1024)S(1)}, /*index=5*/f32[1024]{0:T(1024)S(1)}, bf16[768,1024]{1,0:T(8,128)(2,1)S(1)}) fusion(bf16[15,1024]{1,0:T(8,128)(2,1)S(1)} %collective-permute-done.1, bf16[768,1024]{1,0:T(8,128)(2,1)} %copy-done.1, ...), kind=kLoop, calls=%fused_computation.196 | loop fusion | flops 36956160 | bytes 9516036 | tf_op jit(solution)/shard_map/reduce_sum | solution.py:50
  205.4 3.0 collective-permute-start.3
  208.4 2.7 fusion.60
  211.1 3.2 fusion.74
  214.4 2.9 fusion.59
  217.3 3.7 fusion.76
  221.0 4.5 fusion.139
  225.5 2.7 stack.127
  228.2 40.0 %multiply_convert_fusion.1 = (bf16[768,1024]{1,0:T(8,128)(2,1)S(1)}, f32[768,1024]{1,0:T(8,128)S(1)}) fusion(f32[768,2048]{1,0:T(8,128)} %copy-done.4, bf16[768,1024]{1,0:T(8,128)(2,1)} %copy-done.3, bf16[15,1024]{1,0:T(8,128)(2,1)S(1)} %collective-permute-done.3, f32[1024]{0:T(1024)S(1)} %bitcast.147, f32[1024]{0:T(1024)S(1)} %bitcast.149, ...), kind=kLoop, calls=%fused_computation.204 | loop fusion | flops 147849216 | bytes 9628672 | tf_op jit(solution)/shard_map/convert
  268.2 4.7 multiply_convert_fusion
  273.0 3.5 convolution_bitcast_fusion
  276.5 8.0 %pad_maximum_fusion = f32[1024,3072]{0,1:T(8,128)} fusion(f32[1024,1024]{0,1:T(8,128)S(1)} %copy-done.6, f32[1024,2048]{0,1:T(8,128)S(1)} %convolution_bitcast_fusion), kind=kLoop, calls=%fused_computation.32 | loop fusion | flops 3145728 | bytes 25165824 | tf_op jit(solution)/shard_map/concatenate | solution.py:114
  284.5 12.6 %copy.19 = f32[1024,3072]{1,0:T(8,128)} copy(f32[1024,3072]{0,1:T(8,128)} %pad_maximum_fusion) | data formatting | bytes 25165824
  297.7 5.4 fusion.146
  303.1 4.6 fusion.145
  307.6 58.1 %all-reduce.4.cloned.1.call-done = f32[31,1024]{1,0:T(8,128)} async-done(((f32[31,1024]{1,0:T(8,128)}), f32[31,1024]{1,0:T(8,128)}) %all-reduce.4.cloned.1.call-update) | async-done | bytes 126992 | tf_op jit(solution)/shard_map/psum | solution.py:104
  367.4 223.3 %reduce-scatter.4.cloned.1.call-done = f32[8,3072]{1,0:T(8,128)} async-done(((f32[1024,3072]{1,0:T(8,128)}), f32[8,3072]{1,0:T(8,128)}) %reduce-scatter.4.cloned.1.call-update) | async-done | bytes 98320
  594.7 2.2 copy.17
  (62 shorter events, 15.7 us)
Async XLA Ops:
  7.2 110.4 %copy-start = (bf16[1024,1024]{1,0:T(8,128)(2,1)S(1)}, bf16[1024,1024]{1,0:T(8,128)(2,1)}, u32[]{:S(2)}) copy-start(bf16[1024,1024]{1,0:T(8,128)(2,1)} %param.14) | copy-start | bytes 6291460
  7.2 358.6 %all-reduce.4.cloned.1.call-start = ((), (), s32[]{:S(2)}) async-start(), calls=%async_computation.1 | async-start | bytes 262144 | tf_op jit(solution)/shard_map/psum | solution.py:104
  13.7 2.7 copy-start.4
  13.7 5.4 copy-start.11
  16.4 6.4 %copy-start.1 = (bf16[768,1024]{1,0:T(8,128)(2,1)}, bf16[768,1024]{1,0:T(8,128)(2,1)S(1)}, u32[]{:S(2)}) copy-start(bf16[768,1024]{1,0:T(8,128)(2,1)S(1)} %multiply_convert_fusion.4) | copy-start | bytes 4718596
  16.4 101.2 %copy-start.12 = (f32[1024]{0:T(1024)S(1)}, f32[1024]{0:T(1024)}, u32[]{:S(2)}) copy-start(f32[1024]{0:T(1024)} %param.12) | copy-start | bytes 12292
  16.4 101.2 %copy-start.16 = (f32[1024]{0:T(1024)S(1)}, f32[1024]{0:T(1024)}, u32[]{:S(2)}) copy-start(f32[1024]{0:T(1024)} %param.13) | copy-start | bytes 12292
  16.4 3.5 collective-permute-start
  17.8 5.0 collective-permute-start.1
  189.0 19.4 %copy-start.2 = (bf16[768,1024]{1,0:T(8,128)(2,1)S(1)}, bf16[768,1024]{1,0:T(8,128)(2,1)}, u32[]{:S(2)}) copy-start(bf16[768,1024]{1,0:T(8,128)(2,1)} %copy-done.1) | copy-start | bytes 4718596
  204.0 13.2 %copy-start.3 = (bf16[768,1024]{1,0:T(8,128)(2,1)}, bf16[768,1024]{1,0:T(8,128)(2,1)S(1)}, u32[]{:S(2)}) copy-start(bf16[768,1024]{1,0:T(8,128)(2,1)S(1)} %get-tuple-element.64) | copy-start | bytes 4718596
  204.1 24.1 %collective-permute-start.2 = (bf16[15,1024]{1,0:T(8,128)(2,1)S(1)}, bf16[15,1024]{1,0:T(8,128)(2,1)S(1)}, u32[]{:S(2)}, u32[]{:S(2)}) collective-permute-start(bf16[15,1024]{1,0:T(8,128)(2,1)S(1)} %get-tuple-element.68), channel_id=1, source_target_pairs={{1,0},{2,1},{3,2},{4,3},{5,4},{6,5},{7,6},{9,8},{10,9},{11,10},{12... | collective-permute-start | bytes 92168 | tf_op jit(solution)/shard_map/ppermute | solution.py:18
  205.4 22.8 %collective-permute-start.3 = (bf16[15,1024]{1,0:T(8,128)(2,1)S(1)}, bf16[15,1024]{1,0:T(8,128)(2,1)S(1)}, u32[]{:S(2)}, u32[]{:S(2)}) collective-permute-start(bf16[15,1024]{1,0:T(8,128)(2,1)S(1)} %get-tuple-element.69), channel_id=1, source_target_pairs={{0,1},{1,2},{2,3},{3,4},{4,5},{5,6},{6,7},{8,9},{9,10},{10,11},{11... | collective-permute-start | bytes 92168 | tf_op jit(solution)/shard_map/ppermute | solution.py:16
  214.3 6.6 %copy-start.5 = (f32[768,1024]{1,0:T(8,128)S(1)}, f32[768,1024]{1,0:T(8,128)}, u32[]{:S(2)}) copy-start(f32[768,1024]{1,0:T(8,128)} %get-tuple-element.67) | copy-start | bytes 9437188
  214.3 6.6 %copy-start.14 = (bf16[1,768,1024]{2,1,0:T(8,128)(2,1)S(1)}, bf16[1,768,1024]{2,1,0:T(8,128)(2,1)}, u32[]{:S(2)}) copy-start(bf16[1,768,1024]{2,1,0:T(8,128)(2,1)} %param.15) | copy-start | bytes 4718596
  228.1 362.5 %reduce-scatter.4.cloned.1.call-start = ((), (), s32[]{:S(2)}) async-start(), calls=%async_computation.2 | async-start | bytes 12681216
  268.2 4.7 copy-start.7
  268.2 4.7 copy-start.15
  272.9 3.5 copy-start.9
  272.9 3.5 copy-start.6
  297.7 5.4 copy-start.8
  297.7 5.4 copy-start.10
  297.7 5.4 copy-start.13
Sparse Core Ops, SparseCore 0:
  228.3 137.4 all-reduce.3
  371.5 219.0 reduce-scatter.3
where the time goes:
time: 604 us
  waiting for transfers between devices  284 us (47%)
  blocking collectives  133 us (22%)
  other arithmetic  111 us (18%)
  matrix products  30 us (5%)
  local copies, waits for them, and re-layouts  22.3 us (4%)
  between operations  15.2 us (3%)
  starting transfers between devices  7.12 us (1%)
    unnamed x3, waiting for transfers between devices  223 us
    psum x1, blocking collectives, local(): lax.psum((local_sum, local_sq, local_count), ('dp', 'tm'))  69.6 us
    psum x1, blocking collectives, local(): lax.psum((jnp.sum(dshift * normed, axis=0), jnp.sum(dshift, axis=0)), ('d...  63.8 us
    psum x1, waiting for transfers between devices, local(): lax.psum(taps_kernel(padded, dconv, kernel_taps, frame_rows), ('dp', 'tm'))  58.1 us
    another operation x2, other arithmetic  44.7 us
    reduce_sum x5, other arithmetic, taps_kernel(): jnp.sum(padded_glu[tap_index:tap_index + frame_count].astype(jnp.float32)...  27.5 us
    reduce_sum x1, other arithmetic, local(): local_sum = jnp.sum(conv_out * live_rows, axis=0)  24.4 us
    dot_general x4, matrix products, row_product(): lax.dot_general(left_rows, right_mat, dim_spec, preferred_element_type=jn...  22 us
  transfers between devices with their start and end apart: 6, of which 3 were waited for; matrix products, arithmetic and copies ran while one was open for 17% of the time, Pallas kernels for 0%

commit v1 on v0

--- a/solution.py
+++ b/solution.py
@@ -94,7 +94,7 @@
     swished = (shifted * act_sig * live_rows).astype(jnp.bfloat16)
     dshift = live_rows * dswish * act_sig * (1.0 + shifted * (1.0 - act_sig))
     sum_gain, sum_bias = lax.psum(
-        (jnp.sum(dshift * normed, axis=0), jnp.sum(dshift, axis=0)), ("dp", "tm")
+        lax.psum((jnp.sum(dshift * normed, axis=0), jnp.sum(dshift, axis=0)), "dp"), "tm"
     )
     dconv = (
         live_rows * bn_gain * inv_std * (dshift - sum_bias / count - normed * sum_gain / count)

time: 604 us -> 589 us (0.975)
  blocking collectives: 133 us -> 121 us
    psum x1 -> x2, blocking collectives: 63.8 us -> 51.3 us  [the longest x1 38.4 us: local(): lax.psum((jnp.sum(dshift * normed, axis=0), jnp.sum(dshift, axis=0)), 'dp')]
where the time goes in v1:
time: 589 us; the launch traced here: 588 us
  waiting for transfers between devices  282 us (48%)
  blocking collectives  121 us (21%)
  other arithmetic  111 us (19%)
  matrix products  30 us (5%)
  local copies, waits for them, and re-layouts  22.3 us (4%)
  between operations  15.2 us (3%)
  starting transfers between devices  7.12 us (1%)
    unnamed x3, waiting for transfers between devices  223 us
    psum x1, blocking collectives, local(): lax.psum((local_sum, local_sq, local_count), ('dp', 'tm'))  69.6 us
    psum x1, waiting for transfers between devices, local(): lax.psum(taps_kernel(padded, dconv, kernel_taps, frame_rows), ('dp', 'tm'))  55.2 us
    another operation x2, other arithmetic  44.6 us
    psum x1, blocking collectives, local(): lax.psum((jnp.sum(dshift * normed, axis=0), jnp.sum(dshift, axis=0)), 'dp')  38.4 us
    reduce_sum x5, other arithmetic, taps_kernel(): jnp.sum(padded_glu[tap_index:tap_index + frame_count].astype(jnp.float32)...  27.5 us
    reduce_sum x1, other arithmetic, local(): local_sum = jnp.sum(conv_out * live_rows, axis=0)  24.4 us
    dot_general x4, matrix products, row_product(): lax.dot_general(left_rows, right_mat, dim_spec, preferred_element_type=jn...  22 us
  transfers between devices with their start and end apart: 6, of which 3 were waited for; matrix products, arithmetic and copies ran while one was open for 17% of the time, Pallas kernels for 0%

profile of v1, /device:TPU:0, one launch (start us, length us, event | category | flops | bytes accessed | tf_op | source)
XLA Modules:
  0.0 588.3 jit_solution(24803567652575419)
XLA Ops:
  8.0 5.7 fusion.143
  19.8 3.0 collective-permute-done.1
  22.8 24.4 %multiply_reduce_fusion.2 = (f32[1024]{0:T(1024)S(1)}, f32[1024]{0:T(1024)S(1)}, f32[768,1024]{1,0:T(8,128)}) fusion(f32[768]{0:T(1024)S(1)} %fusion.147, bf16[15,1024]{1,0:T(8,128)(2,1)S(1)} %collective-permute-done.1, bf16[768,1024]{1,0:T(8,128)(2,1)S(1)} %multiply_convert_fusion.4, f32[1024]{0:T(1024)S(1)} %bitcast.146, f32[1024]{0:T(1024)S(1)} %bitcast.148, ...), kind=kLoop, calls=%fused_computation.213 | loop fusion | flops 147060736 | bytes 4918272 | tf_op jit(solution)/shard_map/reduce_sum | solution.py:84
  47.2 69.6 %all-reduce = (f32[1024]{0:T(1024)S(1)}, f32[]{:T(128)}, f32[1024]{0:T(1024)S(1)}) all-reduce(f32[1024]{0:T(1024)S(1)} %get-tuple-element.52, f32[]{:T(128)} %fusion.148, f32[1024]{0:T(1024)S(1)} %get-tuple-element.51), channel_id=1, replica_groups=mesh['dp'=16,'tm'=8] {'dp','tm'}, use_global_device_ids=true, to_apply=%region_5.0 | all-reduce | flops 2049 | bytes 16392 | tf_op jit(solution)/shard_map/psum | solution.py:87
  117.5 6.4 %fusion.151 = (f32[1024]{0:T(1024)S(1)}, f32[1024]{0:T(1024)S(1)}, f32[768,1024]{1,0:T(8,128)}) fusion(f32[1024]{0:T(1024)S(1)} %get-tuple-element.108, f32[768,1024]{1,0:T(8,128)} %get-tuple-element.69, f32[1024]{0:T(1024)S(1)} %get-tuple-element.107, f32[1024]{0:T(1024)S(1)} %copy-done.16, f32[1024]{0:T(1024)S(1)} %copy-done.12, ...), kind=kOutput, calls=%fused_computation.316 | convolution fusion | flops 1623193600 | bytes 9989120 | tf_op jit(solution)/shard_map/dot_general | solution.py:60
  124.0 38.4 %all-reduce.1 = (f32[1024]{0:T(1024)S(1)}, f32[1024]{0:T(1024)S(1)}) all-reduce(f32[1024]{0:T(1024)S(1)} %get-tuple-element.58, f32[1024]{0:T(1024)S(1)} %get-tuple-element.57), channel_id=1, replica_groups=mesh['dp'=16,'tm'=8] {'dp'}, use_global_device_ids=true, to_apply=%region_10.0 | all-reduce | flops 2048 | bytes 16384 | tf_op jit(solution)/shard_map/psum | solution.py:97
  162.4 12.9 %all-reduce.2 = (f32[1024]{0:T(1024)S(1)}, f32[1024]{0:T(1024)S(1)}) all-reduce(f32[1024]{0:T(1024)S(1)} %get-tuple-element.62, f32[1024]{0:T(1024)S(1)} %get-tuple-element.63), channel_id=1, replica_groups=mesh['dp'=16,'tm'=8] {'tm'}, use_global_device_ids=true, to_apply=%region_11.0 | all-reduce | flops 2048 | bytes 16384 | tf_op jit(solution)/shard_map/psum | solution.py:96
  176.5 15.0 %fusion.75 = (f32[1024]{0:T(1024)S(1)}, f32[1024]{0:T(1024)S(1)}, f32[1024]{0:T(1024)S(1)}, f32[1024]{0:T(1024)S(1)}, f32[1024]{0:T(1024)S(1)}, /*index=5*/f32[1024]{0:T(1024)S(1)}, bf16[768,1024]{1,0:T(8,128)(2,1)S(1)}) fusion(bf16[15,1024]{1,0:T(8,128)(2,1)S(1)} %collective-permute-done.1, bf16[768,1024]{1,0:T(8,128)(2,1)} %copy-done.1, ...), kind=kLoop, calls=%fused_computation.196 | loop fusion | flops 36956160 | bytes 9516036 | tf_op jit(solution)/shard_map/reduce_sum | solution.py:50
  192.9 3.0 collective-permute-start.3
  195.9 2.7 fusion.60
  198.6 3.2 fusion.74
  201.8 2.9 fusion.59
  204.7 3.7 fusion.76
  208.5 4.5 fusion.139
  212.9 2.7 stack.127
  215.7 40.0 %multiply_convert_fusion.1 = (bf16[768,1024]{1,0:T(8,128)(2,1)S(1)}, f32[768,1024]{1,0:T(8,128)S(1)}) fusion(f32[768,2048]{1,0:T(8,128)} %copy-done.4, bf16[768,1024]{1,0:T(8,128)(2,1)} %copy-done.3, bf16[15,1024]{1,0:T(8,128)(2,1)S(1)} %collective-permute-done.3, f32[1024]{0:T(1024)S(1)} %bitcast.147, f32[1024]{0:T(1024)S(1)} %bitcast.149, ...), kind=kLoop, calls=%fused_computation.204 | loop fusion | flops 147849216 | bytes 9628672 | tf_op jit(solution)/shard_map/convert
  255.7 4.7 multiply_convert_fusion
  260.4 3.5 convolution_bitcast_fusion
  263.9 8.0 %pad_maximum_fusion = f32[1024,3072]{0,1:T(8,128)} fusion(f32[1024,1024]{0,1:T(8,128)S(1)} %copy-done.6, f32[1024,2048]{0,1:T(8,128)S(1)} %convolution_bitcast_fusion), kind=kLoop, calls=%fused_computation.32 | loop fusion | flops 3145728 | bytes 25165824 | tf_op jit(solution)/shard_map/concatenate | solution.py:114
  272.0 12.6 %copy.19 = f32[1024,3072]{1,0:T(8,128)} copy(f32[1024,3072]{0,1:T(8,128)} %pad_maximum_fusion) | data formatting | bytes 25165824
  285.2 5.4 fusion.146
  290.6 4.6 fusion.145
  295.1 55.2 %all-reduce.5.cloned.1.call-done = f32[31,1024]{1,0:T(8,128)} async-done(((f32[31,1024]{1,0:T(8,128)}), f32[31,1024]{1,0:T(8,128)}) %all-reduce.5.cloned.1.call-update) | async-done | bytes 126992 | tf_op jit(solution)/shard_map/psum | solution.py:104
  351.9 223.3 %reduce-scatter.4.cloned.1.call-done = f32[8,3072]{1,0:T(8,128)} async-done(((f32[1024,3072]{1,0:T(8,128)}), f32[8,3072]{1,0:T(8,128)}) %reduce-scatter.4.cloned.1.call-update) | async-done | bytes 98320
  (63 shorter events, 17.8 us)
Async XLA Ops:
  7.2 110.4 %copy-start = (bf16[1024,1024]{1,0:T(8,128)(2,1)S(1)}, bf16[1024,1024]{1,0:T(8,128)(2,1)}, u32[]{:S(2)}) copy-start(bf16[1024,1024]{1,0:T(8,128)(2,1)} %param.14) | copy-start | bytes 6291460
  7.2 343.2 %all-reduce.5.cloned.1.call-start = ((), (), s32[]{:S(2)}) async-start(), calls=%async_computation.1 | async-start | bytes 262144 | tf_op jit(solution)/shard_map/psum | solution.py:104
  13.7 2.7 copy-start.4
  13.7 5.4 copy-start.11
  16.4 6.4 %copy-start.1 = (bf16[768,1024]{1,0:T(8,128)(2,1)}, bf16[768,1024]{1,0:T(8,128)(2,1)S(1)}, u32[]{:S(2)}) copy-start(bf16[768,1024]{1,0:T(8,128)(2,1)S(1)} %multiply_convert_fusion.4) | copy-start | bytes 4718596
  16.4 101.2 %copy-start.12 = (f32[1024]{0:T(1024)S(1)}, f32[1024]{0:T(1024)}, u32[]{:S(2)}) copy-start(f32[1024]{0:T(1024)} %param.12) | copy-start | bytes 12292
  16.4 101.2 %copy-start.16 = (f32[1024]{0:T(1024)S(1)}, f32[1024]{0:T(1024)}, u32[]{:S(2)}) copy-start(f32[1024]{0:T(1024)} %param.13) | copy-start | bytes 12292
  16.4 3.5 collective-permute-start
  17.8 5.0 collective-permute-start.1
  176.5 19.4 %copy-start.2 = (bf16[768,1024]{1,0:T(8,128)(2,1)S(1)}, bf16[768,1024]{1,0:T(8,128)(2,1)}, u32[]{:S(2)}) copy-start(bf16[768,1024]{1,0:T(8,128)(2,1)} %copy-done.1) | copy-start | bytes 4718596
  191.5 13.2 %copy-start.3 = (bf16[768,1024]{1,0:T(8,128)(2,1)}, bf16[768,1024]{1,0:T(8,128)(2,1)S(1)}, u32[]{:S(2)}) copy-start(bf16[768,1024]{1,0:T(8,128)(2,1)S(1)} %get-tuple-element.66) | copy-start | bytes 4718596
  191.6 24.1 %collective-permute-start.2 = (bf16[15,1024]{1,0:T(8,128)(2,1)S(1)}, bf16[15,1024]{1,0:T(8,128)(2,1)S(1)}, u32[]{:S(2)}, u32[]{:S(2)}) collective-permute-start(bf16[15,1024]{1,0:T(8,128)(2,1)S(1)} %get-tuple-element.70), channel_id=1, source_target_pairs={{1,0},{2,1},{3,2},{4,3},{5,4},{6,5},{7,6},{9,8},{10,9},{11,10},{12... | collective-permute-start | bytes 92168 | tf_op jit(solution)/shard_map/ppermute | solution.py:18
  192.9 22.8 %collective-permute-start.3 = (bf16[15,1024]{1,0:T(8,128)(2,1)S(1)}, bf16[15,1024]{1,0:T(8,128)(2,1)S(1)}, u32[]{:S(2)}, u32[]{:S(2)}) collective-permute-start(bf16[15,1024]{1,0:T(8,128)(2,1)S(1)} %get-tuple-element.71), channel_id=1, source_target_pairs={{0,1},{1,2},{2,3},{3,4},{4,5},{5,6},{6,7},{8,9},{9,10},{10,11},{11... | collective-permute-start | bytes 92168 | tf_op jit(solution)/shard_map/ppermute | solution.py:16
  201.8 6.6 %copy-start.5 = (f32[768,1024]{1,0:T(8,128)S(1)}, f32[768,1024]{1,0:T(8,128)}, u32[]{:S(2)}) copy-start(f32[768,1024]{1,0:T(8,128)} %get-tuple-element.69) | copy-start | bytes 9437188
  201.8 6.6 %copy-start.14 = (bf16[1,768,1024]{2,1,0:T(8,128)(2,1)S(1)}, bf16[1,768,1024]{2,1,0:T(8,128)(2,1)}, u32[]{:S(2)}) copy-start(bf16[1,768,1024]{2,1,0:T(8,128)(2,1)} %param.15) | copy-start | bytes 4718596
  215.6 359.6 %reduce-scatter.4.cloned.1.call-start = ((), (), s32[]{:S(2)}) async-start(), calls=%async_computation.2 | async-start | bytes 12681216
  255.7 4.7 copy-start.7
  255.7 4.7 copy-start.15
  260.4 3.5 copy-start.9
  260.4 3.5 copy-start.6
  285.2 5.4 copy-start.8
  285.2 5.4 copy-start.10
  285.2 5.4 copy-start.13
Sparse Core Ops, SparseCore 0:
  215.7 134.5 all-reduce.4
  356.1 219.0 reduce-scatter.3
